TPU v7x, 128 devices: a whole 4x4x4 slice. The times are simulated.
128 devices in a mesh: wide: 16 (over x, z), narrow: 8 (over y, core).
Axes of the slice: x: 4, y: 4, z: 4, core: 2. Of those that a mesh axis runs over, the one named last changes fastest.
Arguments:
- tensor_slab: float32 [512, 512, 2048], P(None, 'wide', 'narrow'), may hold values from -220 to 220
- start_basis: float32 [512, 64], replicated, may hold values from -6 to 6
Outputs:
- factor_basis: float32 [512, 64], replicated
- core_unfold: float32 [2048, 64, 512], P('narrow', 'wide')
All inputs are finite; a program needn't handle non-finite values.
Results may differ from a plain program's by a relative error of at most 0.0003.
Values sent between devices are 32-bit elements; how exact they have to be, the bound alone decides.
A program may use at most 64 MiB of HBM per device.

v0:
```python
import functools

import jax
import jax.numpy as jnp
from jax import lax
from jax.experimental import pallas as pl
from jax.experimental.pallas import tpu as pltpu
from jax.sharding import PartitionSpec as P

I1 = 512
ITERS = 8
MESH = pl.DeviceIdType.MESH


def orthonormal(block, inner):
    lower_factor = jnp.linalg.cholesky(inner)
    return jax.scipy.linalg.solve_triangular(lower_factor, block.T, lower=True).T


def _allreduce_kernel(x_ref, o_ref, acc1, acc2, acc3, acc4, r1, r2, r3, r4, full, send_sems, recv_sems):
    w = lax.axis_index("wide")
    n = lax.axis_index("narrow")
    px, pz = w // 4, w % 4
    py, pc = n // 2, n % 2
    rows, cols = x_ref.shape
    h1 = rows // 2
    h2 = h1 // 4
    h3 = h2 // 4
    cw = cols // 4

    core_dev = (w, py * 2 + (1 - pc))

    def y_dev(o):
        return (w, ((py + o) % 4) * 2 + pc)

    def x_dev(o):
        return (((px + o) % 4) * 4 + pz, n)

    def z_dev(o):
        return (px * 4 + (pz + o) % 4, n)

    partners = [core_dev] + [y_dev(o) for o in (1, 2, 3)] + [x_dev(o) for o in (1, 2, 3)] + [z_dev(o) for o in (1, 2, 3)]
    barrier = pltpu.get_barrier_semaphore()
    for dev in partners:
        pl.semaphore_signal(barrier, inc=1, device_id=dev, device_id_type=MESH)
    pl.semaphore_wait(barrier, len(partners))

    slot = [0]

    def send(src, dst, dev):
        k = slot[0]
        slot[0] += 1
        cp = pltpu.make_async_remote_copy(
            src_ref=src, dst_ref=dst, send_sem=send_sems.at[k], recv_sem=recv_sems.at[k],
            device_id=dev, device_id_type=MESH)
        cp.start()
        return cp

    def wait_all(cps):
        for cp in cps:
            cp.wait()

    cp = send(x_ref.at[pl.ds(pl.multiple_of((1 - pc) * h1, 8), h1)], r1, core_dev)
    cp.wait()
    acc1[...] = x_ref[pl.ds(pl.multiple_of(pc * h1, 8), h1), :] + r1[...]

    cps = []
    for o in (1, 2, 3):
        q = (py + o) % 4
        cps.append(send(acc1.at[pl.ds(pl.multiple_of(q * h2, 8), h2)], r2.at[o - 1], y_dev(o)))
    wait_all(cps)
    acc2[...] = acc1[pl.ds(pl.multiple_of(py * h2, 8), h2), :] + r2[0] + r2[1] + r2[2]

    cps = []
    for o in (1, 2, 3):
        q = (px + o) % 4
        cps.append(send(acc2.at[pl.ds(pl.multiple_of(q * h3, 8), h3)], r3.at[o - 1], x_dev(o)))
    wait_all(cps)
    acc3[...] = acc2[pl.ds(pl.multiple_of(px * h3, 8), h3), :] + r3[0] + r3[1] + r3[2]

    cps = []
    for o in (1, 2, 3):
        q = (pz + o) % 4
        cps.append(send(acc3.at[:, pl.ds(pl.multiple_of(q * cw, 128), cw)], r4.at[o - 1], z_dev(o)))
    wait_all(cps)
    acc4[...] = acc3[:, pl.ds(pl.multiple_of(pz * cw, 128), cw)] + r4[0] + r4[1] + r4[2]

    row1 = pc * h1
    row2 = row1 + py * h2
    row3 = row2 + px * h3
    full[pl.ds(pl.multiple_of(row3, 8), h3), pl.ds(pl.multiple_of(pz * cw, 128), cw)] = acc4[...]

    mine = full.at[pl.ds(pl.multiple_of(row3, 8), h3), pl.ds(pl.multiple_of(pz * cw, 128), cw)]
    wait_all([send(mine, mine, z_dev(o)) for o in (1, 2, 3)])
    mine = full.at[pl.ds(pl.multiple_of(row3, 8), h3)]
    wait_all([send(mine, mine, x_dev(o)) for o in (1, 2, 3)])
    mine = full.at[pl.ds(pl.multiple_of(row2, 8), h2)]
    wait_all([send(mine, mine, y_dev(o)) for o in (1, 2, 3)])
    mine = full.at[pl.ds(pl.multiple_of(row1, 8), h1)]
    send(mine, mine, core_dev).wait()

    o_ref[...] = full[...]


def allreduce_all(x):
    rows, cols = x.shape
    h1 = rows // 2
    h2 = h1 // 4
    h3 = h2 // 4
    cw = cols // 4
    f32 = jnp.float32
    return pl.pallas_call(
        _allreduce_kernel,
        out_shape=jax.ShapeDtypeStruct((rows, cols), f32),
        in_specs=[pl.BlockSpec(memory_space=pltpu.VMEM)],
        out_specs=pl.BlockSpec(memory_space=pltpu.VMEM),
        scratch_shapes=[
            pltpu.VMEM((h1, cols), f32),
            pltpu.VMEM((h2, cols), f32),
            pltpu.VMEM((h3, cols), f32),
            pltpu.VMEM((h3, cw), f32),
            pltpu.VMEM((h1, cols), f32),
            pltpu.VMEM((3, h2, cols), f32),
            pltpu.VMEM((3, h3, cols), f32),
            pltpu.VMEM((3, h3, cw), f32),
            pltpu.VMEM((rows, cols), f32),
            pltpu.SemaphoreType.DMA((20,)),
            pltpu.SemaphoreType.DMA((20,)),
        ],
        compiler_params=pltpu.CompilerParams(collective_id=0, has_side_effects=True),
    )(x)


def _subspace_kernel(g_ref, b0_ref, o_ref):
    highest = lax.Precision.HIGHEST
    rank = b0_ref.shape[0]
    rows = lax.broadcasted_iota(jnp.int32, (rank, rank), 0)
    cols = lax.broadcasted_iota(jnp.int32, (rank, rank), 1)
    col_idx = lax.broadcasted_iota(jnp.int32, (rank, 1), 0)
    row_idx = lax.broadcasted_iota(jnp.int32, (1, rank), 1)
    eye = jnp.where(rows == cols, 1.0, 0.0).astype(jnp.float32)
    zero = jnp.zeros((rank, rank), jnp.float32)

    def step(j, carry):
        m, e, z = carry
        at_row = rows == j
        row_m = jnp.sum(jnp.where(at_row, m, 0.0), axis=0, keepdims=True)
        col_m = jnp.sum(jnp.where(cols == j, m, 0.0), axis=1, keepdims=True)
        d = jnp.sum(jnp.where(row_idx == j, row_m, 0.0), axis=1, keepdims=True)
        s = lax.rsqrt(d)
        c = jnp.where(col_idx >= j, col_m * s, 0.0)
        r = jnp.where(row_idx >= j, row_m * s, 0.0)
        m = m - c * r
        zr = jnp.sum(jnp.where(at_row, e, 0.0), axis=0, keepdims=True) * s
        e = e - c * zr
        z = jnp.where(at_row, zr, z)
        return m, e, z

    def sweep(_, basis_t):
        block_t = jnp.dot(basis_t, g_ref[...], precision=highest, preferred_element_type=jnp.float32)
        inner = lax.dot_general(block_t, block_t, (((1,), (1,)), ((), ())), precision=highest,
                                preferred_element_type=jnp.float32)
        _, _, l_inv = lax.fori_loop(0, rank, step, (inner, eye, zero))
        return jnp.dot(l_inv, block_t, precision=highest, preferred_element_type=jnp.float32)

    o_ref[...] = lax.fori_loop(0, ITERS, sweep, b0_ref[...])


def subspace_iterate(gram, start_basis):
    basis_t = pl.pallas_call(
        _subspace_kernel,
        out_shape=jax.ShapeDtypeStruct(start_basis.shape[::-1], jnp.float32),
        in_specs=[pl.BlockSpec(memory_space=pltpu.VMEM)] * 2,
        out_specs=pl.BlockSpec(memory_space=pltpu.VMEM),
    )(gram, start_basis.T)
    return basis_t.T


def shards(tensor_slab, start_basis):
    highest = lax.Precision.HIGHEST
    high = lax.Precision.HIGH
    unfold = tensor_slab.reshape(I1, -1)
    basis = start_basis
    local_gram = jnp.dot(unfold, unfold.T, precision=high, preferred_element_type=jnp.float32)
    gram_full = allreduce_all(local_gram)
    basis = subspace_iterate(gram_full, start_basis)
    proj = jnp.einsum("ir,ijl->rjl", basis, tensor_slab, precision=high, preferred_element_type=jnp.float32)
    proj = lax.all_to_all(proj, "wide", split_axis=0, concat_axis=1, tiled=True)
    core_unfold = jnp.transpose(proj, (2, 0, 1))
    return (basis, core_unfold)


def solution(mesh):
    placed = (P(None, "wide", "narrow"), P())
    return jax.shard_map(
        shards,
        mesh=mesh,
        in_specs=placed,
        out_specs=(P(), P("narrow", "wide", None)),
        check_vma=False,
    )
```

profile of v0, /device:TPU:0, one launch (start us, length us, event | category | flops | bytes accessed | tf_op | source)
XLA Modules:
  0.0 210.9 jit_solution(16336218354302948757)
XLA Ops:
  0.6 43.0 %fusion.4.x_ref = f32[512,512]{1,0:T(8,128)} fusion(f32[512,32,256]{2,1,0:T(8,128)} %param.2), kind=kOutput, calls=%fused_computation.4 | convolution fusion | flops 12884901888 | bytes 17825792 | tf_op jit(solution)/shard_map/dot_general | solution.py:184
  43.7 41.6 %shard_map.41.g_ref = f32[512,512]{1,0:T(8,128)} custom-call(f32[512,512]{1,0:T(8,128)} %fusion.4.x_ref), custom_call_target="tpu_custom_call" | custom-call | tf_op jit(solution)/shard_map/pallas_call | solution.py:112
  85.3 68.5 %shard_map.42 = f32[64,512]{1,0:T(8,128)} custom-call(f32[512,512]{1,0:T(8,128)} %shard_map.41.g_ref, f32[64,512]{1,0:T(8,128)} %bitcast.16), custom_call_target="tpu_custom_call" | custom-call | tf_op jit(solution)/shard_map/pallas_call | solution.py:170
  153.8 20.1 %fusion = f32[64,32,256]{2,0,1:T(8,128)S(1)} fusion(f32[512,32,256]{2,1,0:T(8,128)} %param.2, f32[64,512]{1,0:T(8,128)} %shard_map.42), kind=kOutput, calls=%fused_computation | convolution fusion | flops 1610612736 | bytes 19005440 | tf_op jit(solution)/shard_map/ir,ijl->rjl/dot_general | solution.py:187
  173.9 1.2 copy.21
  175.1 33.7 %all_to_all.18 = f32[64,32,256]{2,1,0:T(8,128)S(1)} all-to-all(f32[64,32,256]{2,1,0:T(8,128)S(1)} %copy.21), channel_id=1, replica_groups=mesh['wide'=16,'narrow'=8] {'wide'}, dimensions={0} | all-to-all | bytes 4194304 | tf_op jit(solution)/shard_map/all_to_all | solution.py:188
  208.8 0.1 copy.22
  209.0 2.0 copy.23
where the time goes:
time: 211 us
  Pallas kernels  110 us (52%)
  matrix products  63.2 us (30%)
  blocking collectives  33.7 us (16%)
  local copies, waits for them, and re-layouts  3.32 us (2%)
    pallas_call x1, Pallas kernels, subspace_iterate(): pl.pallas_call(_subspace_kernel, out_shape=jax.ShapeDtypeStruct(start_bas...  68.5 us
    dot_general x1, matrix products, shards(): jnp.dot(unfold, unfold.T, precision=high, preferred_element_type=jnp.floa...  43 us
    pallas_call x1, Pallas kernels, allreduce_all(): pl.pallas_call(_allreduce_kernel, out_shape=jax.ShapeDtypeStruct((rows, c...  41.6 us
    all_to_all x1, blocking collectives, shards(): proj = lax.all_to_all(proj, 'wide', split_axis=0, concat_axis=1, tiled=True)  33.7 us
    dot_general x1, matrix products, shards(): jnp.einsum('ir,ijl->rjl', basis, tensor_slab, precision=high, preferred_e...  20.1 us

commit v1 on v0

--- a/solution.py
+++ b/solution.py
@@ -176,13 +176,57 @@
     return basis_t.T
 
 
+def _gram_kernel(s_ref, o_ref, hi_ref, lo_ref, cross_ref):
+    step = pl.program_id(0)
+    depth = s_ref.shape[1]
+    width = s_ref.shape[2]
+    for jj in range(depth):
+        x = s_ref[:, jj, :]
+        hi = x.astype(jnp.bfloat16)
+        lo = (x - hi.astype(jnp.float32)).astype(jnp.bfloat16)
+        hi_ref[:, jj * width:(jj + 1) * width] = hi
+        lo_ref[:, jj * width:(jj + 1) * width] = lo
+    nt = (((1,), (1,)), ((), ()))
+    hh = lax.dot_general(hi_ref[...], hi_ref[...], nt, preferred_element_type=jnp.float32)
+    hl = lax.dot_general(hi_ref[...], lo_ref[...], nt, preferred_element_type=jnp.float32)
+
+    @pl.when(step == 0)
+    def _():
+        o_ref[...] = hh
+        cross_ref[...] = hl
+
+    @pl.when(step > 0)
+    def _():
+        o_ref[...] += hh
+        cross_ref[...] += hl
+
+    @pl.when(step == pl.num_programs(0) - 1)
+    def _():
+        o_ref[...] += cross_ref[...] + cross_ref[...].T
+
+
+def local_gram(slab, depth=8):
+    rows, cols, width = slab.shape
+    return pl.pallas_call(
+        _gram_kernel,
+        out_shape=jax.ShapeDtypeStruct((rows, rows), jnp.float32),
+        grid=(cols // depth,),
+        in_specs=[pl.BlockSpec((rows, depth, width), lambda g: (0, g, 0))],
+        out_specs=pl.BlockSpec((rows, rows), lambda g: (0, 0)),
+        scratch_shapes=[
+            pltpu.VMEM((rows, depth * width), jnp.bfloat16),
+            pltpu.VMEM((rows, depth * width), jnp.bfloat16),
+            pltpu.VMEM((rows, rows), jnp.float32),
+        ],
+        compiler_params=pltpu.CompilerParams(vmem_limit_bytes=48 * 1024 * 1024),
+    )(slab)
+
+
 def shards(tensor_slab, start_basis):
     highest = lax.Precision.HIGHEST
     high = lax.Precision.HIGH
-    unfold = tensor_slab.reshape(I1, -1)
     basis = start_basis
-    local_gram = jnp.dot(unfold, unfold.T, precision=high, preferred_element_type=jnp.float32)
-    gram_full = allreduce_all(local_gram)
+    gram_full = allreduce_all(local_gram(tensor_slab))
     basis = subspace_iterate(gram_full, start_basis)
     proj = jnp.einsum("ir,ijl->rjl", basis, tensor_slab, precision=high, preferred_element_type=jnp.float32)
     proj = lax.all_to_all(proj, "wide", split_axis=0, concat_axis=1, tiled=True)

time: 211 us -> 226 us (1.071)
  Pallas kernels: 110 us -> 167 us
  matrix products: 63.2 us -> 20.1 us
    pallas_call x0 -> x1, Pallas kernels: none -> 56.8 us  [local_gram(): pl.pallas_call(_gram_kernel, out_shape=jax.ShapeDtypeStruct((rows, rows),...]
    dot_general x1 -> x0, matrix products: 43 us -> none  [shards(): jnp.dot(unfold, unfold.T, precision=high, preferred_element_type=jnp.floa...]
where the time goes in v1:
time: 226 us
  Pallas kernels  167 us (74%)
  blocking collectives  33.7 us (15%)
  matrix products  20.1 us (9%)
  local copies, waits for them, and re-layouts  4.29 us (2%)
    pallas_call x1, Pallas kernels, subspace_iterate(): pl.pallas_call(_subspace_kernel, out_shape=jax.ShapeDtypeStruct(start_bas...  68.5 us
    pallas_call x1, Pallas kernels, local_gram(): pl.pallas_call(_gram_kernel, out_shape=jax.ShapeDtypeStruct((rows, rows),...  56.8 us
    pallas_call x1, Pallas kernels, allreduce_all(): pl.pallas_call(_allreduce_kernel, out_shape=jax.ShapeDtypeStruct((rows, c...  41.6 us
    all_to_all x1, blocking collectives, shards(): proj = lax.all_to_all(proj, 'wide', split_axis=0, concat_axis=1, tiled=True)  33.7 us
    dot_general x1, matrix products, shards(): jnp.einsum('ir,ijl->rjl', basis, tensor_slab, precision=high, preferred_e...  20.1 us

profile of v1, /device:TPU:0, one launch (start us, length us, event | category | flops | bytes accessed | tf_op | source)
XLA Modules:
  0.0 225.7 jit_solution(15526449215082983753)
XLA Ops:
  0.6 56.8 %shard_map.41.x_ref = f32[512,512]{1,0:T(8,128)S(1)} custom-call(f32[512,32,256]{2,1,0:T(8,128)} %s_ref.1), custom_call_target="tpu_custom_call" | custom-call | tf_op jit(solution)/shard_map/pallas_call | solution.py:210
  57.4 0.0 copy-start
  57.5 1.0 copy-done
  58.4 41.6 %shard_map.42.g_ref = f32[512,512]{1,0:T(8,128)} custom-call(f32[512,512]{1,0:T(8,128)} %copy-done), custom_call_target="tpu_custom_call" | custom-call | tf_op jit(solution)/shard_map/pallas_call | solution.py:112
  100.0 68.5 %shard_map.43 = f32[64,512]{1,0:T(8,128)} custom-call(f32[512,512]{1,0:T(8,128)} %shard_map.42.g_ref, f32[64,512]{1,0:T(8,128)} %bitcast.14), custom_call_target="tpu_custom_call" | custom-call | tf_op jit(solution)/shard_map/pallas_call | solution.py:170
  168.5 20.1 %fusion = f32[64,32,256]{2,0,1:T(8,128)S(1)} fusion(f32[512,32,256]{2,1,0:T(8,128)} %s_ref.1, f32[64,512]{1,0:T(8,128)} %shard_map.43), kind=kOutput, calls=%fused_computation | convolution fusion | flops 1610612736 | bytes 19005440 | tf_op jit(solution)/shard_map/ir,ijl->rjl/dot_general | solution.py:231
  188.6 1.2 copy.13
  189.9 33.7 %all_to_all.18 = f32[64,32,256]{2,1,0:T(8,128)S(1)} all-to-all(f32[64,32,256]{2,1,0:T(8,128)S(1)} %copy.13), channel_id=1, replica_groups=mesh['wide'=16,'narrow'=8] {'wide'}, dimensions={0} | all-to-all | bytes 4194304 | tf_op jit(solution)/shard_map/all_to_all | solution.py:232
  223.6 0.1 copy.14
  223.7 2.0 copy.15
Async XLA Ops:
  57.4 1.0 copy-start

commit v2 on v0

--- a/solution.py
+++ b/solution.py
@@ -176,13 +176,61 @@
     return basis_t.T
 
 
+def _gram_kernel(s_hbm, o_ref, buf, hi_ref, lo_ref, cross_ref, sems):
+    _, cols, width = s_hbm.shape
+    slots = buf.shape[0]
+    depth = hi_ref.shape[1] // width
+
+    def copy(j):
+        return pltpu.make_async_copy(s_hbm.at[:, j, :], buf.at[j % slots], sems.at[j % slots])
+
+    for j in range(slots - 1):
+        copy(j).start()
+    nt = (((1,), (1,)), ((), ()))
+    for g in range(cols // depth):
+        for jj in range(depth):
+            j = g * depth + jj
+            if j + slots - 1 < cols:
+                copy(j + slots - 1).start()
+            copy(j).wait()
+            x = buf[j % slots]
+            hi = x.astype(jnp.bfloat16)
+            lo = (x - hi.astype(jnp.float32)).astype(jnp.bfloat16)
+            hi_ref[:, jj * width:(jj + 1) * width] = hi
+            lo_ref[:, jj * width:(jj + 1) * width] = lo
+        hh = lax.dot_general(hi_ref[...], hi_ref[...], nt, preferred_element_type=jnp.float32)
+        hl = lax.dot_general(hi_ref[...], lo_ref[...], nt, preferred_element_type=jnp.float32)
+        if g == 0:
+            o_ref[...] = hh
+            cross_ref[...] = hl
+        else:
+            o_ref[...] += hh
+            cross_ref[...] += hl
+    o_ref[...] += cross_ref[...] + cross_ref[...].T
+
+
+def local_gram(slab, depth=8, slots=8):
+    rows, cols, width = slab.shape
+    return pl.pallas_call(
+        _gram_kernel,
+        out_shape=jax.ShapeDtypeStruct((rows, rows), jnp.float32),
+        in_specs=[pl.BlockSpec(memory_space=pl.ANY)],
+        out_specs=pl.BlockSpec(memory_space=pltpu.VMEM),
+        scratch_shapes=[
+            pltpu.VMEM((slots, rows, width), jnp.float32),
+            pltpu.VMEM((rows, depth * width), jnp.bfloat16),
+            pltpu.VMEM((rows, depth * width), jnp.bfloat16),
+            pltpu.VMEM((rows, rows), jnp.float32),
+            pltpu.SemaphoreType.DMA((slots,)),
+        ],
+        compiler_params=pltpu.CompilerParams(vmem_limit_bytes=48 * 1024 * 1024),
+    )(slab)
+
 def shards(tensor_slab, start_basis):
     highest = lax.Precision.HIGHEST
     high = lax.Precision.HIGH
-    unfold = tensor_slab.reshape(I1, -1)
     basis = start_basis
-    local_gram = jnp.dot(unfold, unfold.T, precision=high, preferred_element_type=jnp.float32)
-    gram_full = allreduce_all(local_gram)
+    gram_full = allreduce_all(local_gram(tensor_slab))
     basis = subspace_iterate(gram_full, start_basis)
     proj = jnp.einsum("ir,ijl->rjl", basis, tensor_slab, precision=high, preferred_element_type=jnp.float32)
     proj = lax.all_to_all(proj, "wide", split_axis=0, concat_axis=1, tiled=True)

time: 211 us -> 183 us (0.87)
  matrix products: 63.2 us -> 20.1 us
  Pallas kernels: 110 us -> 124 us
    dot_general x1 -> x0, matrix products: 43 us -> none  [shards(): jnp.dot(unfold, unfold.T, precision=high, preferred_element_type=jnp.floa...]
    pallas_call x0 -> x1, Pallas kernels: none -> 14.3 us  [local_gram(): pl.pallas_call(_gram_kernel, out_shape=jax.ShapeDtypeStruct((rows, rows),...]
where the time goes in v2:
time: 183 us
  Pallas kernels  124 us (68%)
  blocking collectives  33.7 us (18%)
  matrix products  20.1 us (11%)
  local copies, waits for them, and re-layouts  4.29 us (2%)
    pallas_call x1, Pallas kernels, subspace_iterate(): pl.pallas_call(_subspace_kernel, out_shape=jax.ShapeDtypeStruct(start_bas...  68.5 us
    pallas_call x1, Pallas kernels, allreduce_all(): pl.pallas_call(_allreduce_kernel, out_shape=jax.ShapeDtypeStruct((rows, c...  41.6 us
    all_to_all x1, blocking collectives, shards(): proj = lax.all_to_all(proj, 'wide', split_axis=0, concat_axis=1, tiled=True)  33.7 us
    dot_general x1, matrix products, shards(): jnp.einsum('ir,ijl->rjl', basis, tensor_slab, precision=high, preferred_e...  20.1 us
    pallas_call x1, Pallas kernels, local_gram(): pl.pallas_call(_gram_kernel, out_shape=jax.ShapeDtypeStruct((rows, rows),...  14.3 us

profile of v2, /device:TPU:0, one launch (start us, length us, event | category | flops | bytes accessed | tf_op | source)
XLA Modules:
  0.0 183.2 jit_solution(14689508841596161802)
XLA Ops:
  0.6 14.3 %shard_map.41.x_ref = f32[512,512]{1,0:T(8,128)S(1)} custom-call(f32[512,32,256]{2,1,0:T(8,128)} %s_hbm.1), custom_call_target="tpu_custom_call" | custom-call | tf_op jit(solution)/shard_map/pallas_call | solution.py:214
  15.0 0.0 copy-start
  15.0 1.0 copy-done
  15.9 41.6 %shard_map.42.g_ref = f32[512,512]{1,0:T(8,128)} custom-call(f32[512,512]{1,0:T(8,128)} %copy-done), custom_call_target="tpu_custom_call" | custom-call | tf_op jit(solution)/shard_map/pallas_call | solution.py:112
  57.5 68.5 %shard_map.43 = f32[64,512]{1,0:T(8,128)} custom-call(f32[512,512]{1,0:T(8,128)} %shard_map.42.g_ref, f32[64,512]{1,0:T(8,128)} %bitcast.14), custom_call_target="tpu_custom_call" | custom-call | tf_op jit(solution)/shard_map/pallas_call | solution.py:170
  126.0 20.1 %fusion = f32[64,32,256]{2,0,1:T(8,128)S(1)} fusion(f32[512,32,256]{2,1,0:T(8,128)} %s_hbm.1, f32[64,512]{1,0:T(8,128)} %shard_map.43), kind=kOutput, calls=%fused_computation | convolution fusion | flops 1610612736 | bytes 19005440 | tf_op jit(solution)/shard_map/ir,ijl->rjl/dot_general | solution.py:235
  146.1 1.2 copy.13
  147.4 33.7 %all_to_all.18 = f32[64,32,256]{2,1,0:T(8,128)S(1)} all-to-all(f32[64,32,256]{2,1,0:T(8,128)S(1)} %copy.13), channel_id=1, replica_groups=mesh['wide'=16,'narrow'=8] {'wide'}, dimensions={0} | all-to-all | bytes 4194304 | tf_op jit(solution)/shard_map/all_to_all | solution.py:236
  181.1 0.1 copy.14
  181.2 2.0 %copy.15 = f32[256,4,512]{2,1,0:T(4,128)} copy(f32[256,4,512]{0,2,1:T(8,128)S(1)} %bitcast.12) | data formatting | bytes 4194304
Async XLA Ops:
  15.0 1.0 copy-start

commit v3 on v2

--- a/solution.py
+++ b/solution.py
@@ -176,18 +176,25 @@
     return basis_t.T
 
 
-def _gram_kernel(s_hbm, o_ref, buf, hi_ref, lo_ref, cross_ref, sems):
+def _gram_kernel(s_hbm, o_ref, hi_hbm, lo_hbm, buf, hi_ref, lo_ref, cross_ref, sems, out_sems):
     _, cols, width = s_hbm.shape
     slots = buf.shape[0]
-    depth = hi_ref.shape[1] // width
+    groups = out_sems.shape[1]
+    span = hi_ref.shape[1] // groups
+    depth = span // width
 
     def copy(j):
         return pltpu.make_async_copy(s_hbm.at[:, j, :], buf.at[j % slots], sems.at[j % slots])
+
+    def write_back(g):
+        part = pl.ds(g * span, span)
+        return (pltpu.make_async_copy(hi_ref.at[:, part], hi_hbm.at[:, part], out_sems.at[0, g]),
+                pltpu.make_async_copy(lo_ref.at[:, part], lo_hbm.at[:, part], out_sems.at[1, g]))
 
     for j in range(slots - 1):
         copy(j).start()
     nt = (((1,), (1,)), ((), ()))
-    for g in range(cols // depth):
+    for g in range(groups):
         for jj in range(depth):
             j = g * depth + jj
             if j + slots - 1 < cols:
@@ -196,10 +203,13 @@
             x = buf[j % slots]
             hi = x.astype(jnp.bfloat16)
             lo = (x - hi.astype(jnp.float32)).astype(jnp.bfloat16)
-            hi_ref[:, jj * width:(jj + 1) * width] = hi
-            lo_ref[:, jj * width:(jj + 1) * width] = lo
-        hh = lax.dot_general(hi_ref[...], hi_ref[...], nt, preferred_element_type=jnp.float32)
-        hl = lax.dot_general(hi_ref[...], lo_ref[...], nt, preferred_element_type=jnp.float32)
+            hi_ref[:, j * width:(j + 1) * width] = hi
+            lo_ref[:, j * width:(j + 1) * width] = lo
+        for cp in write_back(g):
+            cp.start()
+        part = pl.ds(g * span, span)
+        hh = lax.dot_general(hi_ref[:, part], hi_ref[:, part], nt, preferred_element_type=jnp.float32)
+        hl = lax.dot_general(hi_ref[:, part], lo_ref[:, part], nt, preferred_element_type=jnp.float32)
         if g == 0:
             o_ref[...] = hh
             cross_ref[...] = hl
@@ -207,41 +217,73 @@
             o_ref[...] += hh
             cross_ref[...] += hl
     o_ref[...] += cross_ref[...] + cross_ref[...].T
+    for g in range(groups):
+        for cp in write_back(g):
+            cp.wait()
 
 
 def local_gram(slab, depth=8, slots=8):
     rows, cols, width = slab.shape
+    groups = cols // depth
+    flat = jax.ShapeDtypeStruct((rows, cols * width), jnp.bfloat16)
     return pl.pallas_call(
         _gram_kernel,
-        out_shape=jax.ShapeDtypeStruct((rows, rows), jnp.float32),
+        out_shape=(jax.ShapeDtypeStruct((rows, rows), jnp.float32), flat, flat),
         in_specs=[pl.BlockSpec(memory_space=pl.ANY)],
-        out_specs=pl.BlockSpec(memory_space=pltpu.VMEM),
+        out_specs=(pl.BlockSpec(memory_space=pltpu.VMEM), pl.BlockSpec(memory_space=pl.ANY),
+                   pl.BlockSpec(memory_space=pl.ANY)),
         scratch_shapes=[
             pltpu.VMEM((slots, rows, width), jnp.float32),
-            pltpu.VMEM((rows, depth * width), jnp.bfloat16),
-            pltpu.VMEM((rows, depth * width), jnp.bfloat16),
+            pltpu.VMEM((rows, cols * width), jnp.bfloat16),
+            pltpu.VMEM((rows, cols * width), jnp.bfloat16),
             pltpu.VMEM((rows, rows), jnp.float32),
             pltpu.SemaphoreType.DMA((slots,)),
+            pltpu.SemaphoreType.DMA((2, groups)),
         ],
-        compiler_params=pltpu.CompilerParams(vmem_limit_bytes=48 * 1024 * 1024),
+        compiler_params=pltpu.CompilerParams(vmem_limit_bytes=56 * 1024 * 1024),
     )(slab)
 
-def shards(tensor_slab, start_basis):
+def _project_kernel(b_ref, xh_ref, xl_ref, o_ref):
+    f32 = jnp.float32
+    b = b_ref[...]
+    bh = b.astype(jnp.bfloat16)
+    bl = (b - bh.astype(f32)).astype(jnp.bfloat16)
+    xh = xh_ref[...]
+    o_ref[...] = (jnp.dot(bh, xh, preferred_element_type=f32) + jnp.dot(bh, xl_ref[...], preferred_element_type=f32)
+                  + jnp.dot(bl, xh, preferred_element_type=f32))
+
+
+def project(basis_t, x_hi, x_lo, tile=1024):
+    rank, rows = basis_t.shape
+    width = x_hi.shape[1]
+    return pl.pallas_call(
+        _project_kernel,
+        out_shape=jax.ShapeDtypeStruct((rank, width), jnp.float32),
+        grid=(width // tile,),
+        in_specs=[pl.BlockSpec((rank, rows), lambda g: (0, 0)),
+                  pl.BlockSpec((rows, tile), lambda g: (0, g)), pl.BlockSpec((rows, tile), lambda g: (0, g))],
+        out_specs=pl.BlockSpec((rank, tile), lambda g: (0, g)),
+    )(basis_t, x_hi, x_lo)
+
+
+def shards(wide, tensor_slab, start_basis):
     highest = lax.Precision.HIGHEST
     high = lax.Precision.HIGH
+    _, cols, depth = tensor_slab.shape
     basis = start_basis
-    gram_full = allreduce_all(local_gram(tensor_slab))
+    gram_part, slab_hi, slab_lo = local_gram(tensor_slab)
+    gram_full = allreduce_all(gram_part)
     basis = subspace_iterate(gram_full, start_basis)
-    proj = jnp.einsum("ir,ijl->rjl", basis, tensor_slab, precision=high, preferred_element_type=jnp.float32)
-    proj = lax.all_to_all(proj, "wide", split_axis=0, concat_axis=1, tiled=True)
-    core_unfold = jnp.transpose(proj, (2, 0, 1))
+    proj = project(basis.T, slab_hi, slab_lo)
+    proj = lax.all_to_all(proj, "wide", split_axis=0, concat_axis=0, tiled=True)
+    core_unfold = proj.reshape(wide, -1, cols, depth).transpose(3, 1, 0, 2).reshape(depth, -1, wide * cols)
     return (basis, core_unfold)
 
 
 def solution(mesh):
     placed = (P(None, "wide", "narrow"), P())
     return jax.shard_map(
-        shards,
+        functools.partial(shards, mesh.shape["wide"]),
         mesh=mesh,
         in_specs=placed,
         out_specs=(P(), P("narrow", "wide", None)),

time: 183 us -> 183 us (level)
  matrix products: 20.1 us -> 0 us
  Pallas kernels: 124 us -> 139 us
  local copies, waits for them, and re-layouts: 4.29 us -> 9.08 us
    dot_general x1 -> x0, matrix products: 20.1 us -> none  [shards(): jnp.einsum('ir,ijl->rjl', basis, tensor_slab, precision=high, preferred_e...]
    pallas_call x1 -> x2, Pallas kernels: 14.3 us -> 28.5 us  [the longest x1 17.5 us: local_gram(): pl.pallas_call(_gram_kernel, out_shape=(jax.ShapeDtypeStruct((rows, rows)...]
    reshape x0 -> x2, local copies, waits for them, and re-layouts: none -> 4.18 us  [shards(): proj.reshape(wide, -1, cols, depth).transpose(3, 1, 0, 2)]
where the time goes in v3:
time: 183 us; the launch traced here: 182 us
  Pallas kernels  139 us (76%)
  blocking collectives  33.8 us (18%)
  local copies, waits for them, and re-layouts  9.08 us (5%)
    pallas_call x1, Pallas kernels, subspace_iterate(): pl.pallas_call(_subspace_kernel, out_shape=jax.ShapeDtypeStruct(start_bas...  68.5 us
    pallas_call x1, Pallas kernels, allreduce_all(): pl.pallas_call(_allreduce_kernel, out_shape=jax.ShapeDtypeStruct((rows, c...  41.7 us
    all_to_all x1, blocking collectives, shards(): proj = lax.all_to_all(proj, 'wide', split_axis=0, concat_axis=0, tiled=True)  33.8 us
    pallas_call x1, Pallas kernels, local_gram(): pl.pallas_call(_gram_kernel, out_shape=(jax.ShapeDtypeStruct((rows, rows)...  17.5 us
    pallas_call x1, Pallas kernels, project(): pl.pallas_call(_project_kernel, out_shape=jax.ShapeDtypeStruct((rank, wid...  11 us
    reshape x2, local copies, waits for them, and re-layouts, shards(): proj.reshape(wide, -1, cols, depth).transpose(3, 1, 0, 2)  4.18 us

profile of v3, /device:TPU:0, one launch (start us, length us, event | category | flops | bytes accessed | tf_op | source)
XLA Modules:
  0.0 182.2 jit_solution(9118344535718002436)
XLA Ops:
  0.6 17.5 %shard_map.41 = (f32[512,512]{1,0:T(8,128)}, bf16[512,8192]{1,0:T(8,128)(2,1)}, bf16[512,8192]{1,0:T(8,128)(2,1)}) custom-call(f32[512,32,256]{2,1,0:T(8,128)} %s_hbm.1), custom_call_target="tpu_custom_call" | custom-call | tf_op jit(solution)/shard_map/pallas_call | solution.py:229
  18.1 41.7 %shard_map.42.g_ref = f32[512,512]{1,0:T(8,128)} custom-call(f32[512,512]{1,0:T(8,128)} %get-tuple-element.5.x_ref), custom_call_target="tpu_custom_call" | custom-call | tf_op jit(solution)/shard_map/pallas_call | solution.py:112
  59.8 68.5 %shard_map.43.b_ref = f32[64,512]{1,0:T(8,128)} custom-call(f32[512,512]{1,0:T(8,128)} %shard_map.42.g_ref, f32[64,512]{1,0:T(8,128)} %bitcast.7), custom_call_target="tpu_custom_call" | custom-call | tf_op jit(solution)/shard_map/pallas_call | solution.py:170
  128.3 11.0 %shard_map.44 = f32[64,8192]{1,0:T(8,128)} custom-call(f32[64,512]{1,0:T(8,128)} %shard_map.43.b_ref, bf16[512,8192]{1,0:T(8,128)(2,1)} %get-tuple-element.6.xh_ref, bf16[512,8192]{1,0:T(8,128)(2,1)} %get-tuple-element.7.xl_ref), custom_call_target="tpu_custom_call" | custom-call | tf_op jit(solution)/shard_map/pallas_call | solution.py:259
  139.3 1.9 %all_to_all.6 = f32[16,4,8192]{2,1,0:T(4,128)S(1)} reshape(f32[64,8192]{1,0:T(8,128)} %shard_map.44) | data formatting | bytes 4194304 | tf_op jit(solution)/shard_map/all_to_all | solution.py:278
  141.2 33.8 %all_to_all.9 = f32[16,4,8192]{2,1,0:T(4,128)} all-to-all(f32[16,4,8192]{2,1,0:T(4,128)S(1)} %all_to_all.6), channel_id=1, replica_groups=mesh['wide'=16,'narrow'=8] {'wide'}, dimensions={0} | all-to-all | bytes 4194304 | tf_op jit(solution)/shard_map/all_to_all | solution.py:278
  175.0 2.7 %reshape.15 = f32[16,4,32,256]{3,2,1,0:T(8,128)S(1)} reshape(f32[16,4,8192]{2,1,0:T(4,128)} %all_to_all.9) | data formatting | bytes 4194304 | tf_op jit(solution)/shard_map/reshape | solution.py:279
  177.7 1.5 copy.7
  179.2 3.0 %copy.6 = f32[256,4,512]{2,1,0:T(4,128)} copy(f32[256,4,512]{0,2,1:T(8,128)} %bitcast.5) | data formatting | bytes 4194304

commit v4 on v3

--- a/solution.py
+++ b/solution.py
@@ -141,26 +141,26 @@
     eye = jnp.where(rows == cols, 1.0, 0.0).astype(jnp.float32)
     zero = jnp.zeros((rank, rank), jnp.float32)
 
-    def step(j, carry):
-        m, e, z = carry
-        at_row = rows == j
-        row_m = jnp.sum(jnp.where(at_row, m, 0.0), axis=0, keepdims=True)
-        col_m = jnp.sum(jnp.where(cols == j, m, 0.0), axis=1, keepdims=True)
-        d = jnp.sum(jnp.where(row_idx == j, row_m, 0.0), axis=1, keepdims=True)
-        s = lax.rsqrt(d)
-        c = jnp.where(col_idx >= j, col_m * s, 0.0)
-        r = jnp.where(row_idx >= j, row_m * s, 0.0)
-        m = m - c * r
-        zr = jnp.sum(jnp.where(at_row, e, 0.0), axis=0, keepdims=True) * s
-        e = e - c * zr
-        z = jnp.where(at_row, zr, z)
-        return m, e, z
+    def cholesky_inverse(m):
+        e = eye
+        z = zero
+        for j in range(rank):
+            row_m = m[j:j + 1, :]
+            col_m = m[:, j:j + 1]
+            s = lax.rsqrt(m[j:j + 1, j:j + 1])
+            c = jnp.where(col_idx >= j, col_m * s, 0.0)
+            r = jnp.where(row_idx >= j, row_m * s, 0.0)
+            m = m - c * r
+            zr = e[j:j + 1, :] * s
+            e = e - c * zr
+            z = jnp.where(rows == j, zr, z)
+        return z
 
     def sweep(_, basis_t):
         block_t = jnp.dot(basis_t, g_ref[...], precision=highest, preferred_element_type=jnp.float32)
         inner = lax.dot_general(block_t, block_t, (((1,), (1,)), ((), ())), precision=highest,
                                 preferred_element_type=jnp.float32)
-        _, _, l_inv = lax.fori_loop(0, rank, step, (inner, eye, zero))
+        l_inv = cholesky_inverse(inner)
         return jnp.dot(l_inv, block_t, precision=highest, preferred_element_type=jnp.float32)
 
     o_ref[...] = lax.fori_loop(0, ITERS, sweep, b0_ref[...])

time: 183 us -> 169 us (0.923)
  Pallas kernels: 139 us -> 125 us
    pallas_call x1, Pallas kernels: 68.5 us -> 54.8 us  [subspace_iterate(): pl.pallas_call(_subspace_kernel, out_shape=jax.ShapeDtypeStruct(start_bas...]
where the time goes in v4:
time: 169 us; the launch traced here: 168 us
  Pallas kernels  125 us (74%)
  blocking collectives  33.8 us (20%)
  local copies, waits for them, and re-layouts  9.08 us (5%)
    pallas_call x1, Pallas kernels, subspace_iterate(): pl.pallas_call(_subspace_kernel, out_shape=jax.ShapeDtypeStruct(start_bas...  54.8 us
    pallas_call x1, Pallas kernels, allreduce_all(): pl.pallas_call(_allreduce_kernel, out_shape=jax.ShapeDtypeStruct((rows, c...  41.7 us
    all_to_all x1, blocking collectives, shards(): proj = lax.all_to_all(proj, 'wide', split_axis=0, concat_axis=0, tiled=True)  33.8 us
    pallas_call x1, Pallas kernels, local_gram(): pl.pallas_call(_gram_kernel, out_shape=(jax.ShapeDtypeStruct((rows, rows)...  17.5 us
    pallas_call x1, Pallas kernels, project(): pl.pallas_call(_project_kernel, out_shape=jax.ShapeDtypeStruct((rank, wid...  11 us
    reshape x2, local copies, waits for them, and re-layouts, shards(): proj.reshape(wide, -1, cols, depth).transpose(3, 1, 0, 2)  4.18 us

profile of v4, /device:TPU:0, one launch (start us, length us, event | category | flops | bytes accessed | tf_op | source)
XLA Modules:
  0.0 168.5 jit_solution(10415833729575313623)
XLA Ops:
  0.6 17.5 %shard_map.41 = (f32[512,512]{1,0:T(8,128)}, bf16[512,8192]{1,0:T(8,128)(2,1)}, bf16[512,8192]{1,0:T(8,128)(2,1)}) custom-call(f32[512,32,256]{2,1,0:T(8,128)} %s_hbm.1), custom_call_target="tpu_custom_call" | custom-call | tf_op jit(solution)/shard_map/pallas_call | solution.py:229
  18.1 41.7 %shard_map.42.g_ref = f32[512,512]{1,0:T(8,128)} custom-call(f32[512,512]{1,0:T(8,128)} %get-tuple-element.5.x_ref), custom_call_target="tpu_custom_call" | custom-call | tf_op jit(solution)/shard_map/pallas_call | solution.py:112
  59.8 54.8 %shard_map.43.b_ref = f32[64,512]{1,0:T(8,128)} custom-call(f32[512,512]{1,0:T(8,128)} %shard_map.42.g_ref, f32[64,512]{1,0:T(8,128)} %bitcast.7), custom_call_target="tpu_custom_call" | custom-call | tf_op jit(solution)/shard_map/pallas_call | solution.py:170
  114.6 11.0 %shard_map.44 = f32[64,8192]{1,0:T(8,128)} custom-call(f32[64,512]{1,0:T(8,128)} %shard_map.43.b_ref, bf16[512,8192]{1,0:T(8,128)(2,1)} %get-tuple-element.6.xh_ref, bf16[512,8192]{1,0:T(8,128)(2,1)} %get-tuple-element.7.xl_ref), custom_call_target="tpu_custom_call" | custom-call | tf_op jit(solution)/shard_map/pallas_call | solution.py:259
  125.6 1.9 %all_to_all.6 = f32[16,4,8192]{2,1,0:T(4,128)S(1)} reshape(f32[64,8192]{1,0:T(8,128)} %shard_map.44) | data formatting | bytes 4194304 | tf_op jit(solution)/shard_map/all_to_all | solution.py:278
  127.5 33.8 %all_to_all.9 = f32[16,4,8192]{2,1,0:T(4,128)} all-to-all(f32[16,4,8192]{2,1,0:T(4,128)S(1)} %all_to_all.6), channel_id=1, replica_groups=mesh['wide'=16,'narrow'=8] {'wide'}, dimensions={0} | all-to-all | bytes 4194304 | tf_op jit(solution)/shard_map/all_to_all | solution.py:278
  161.3 2.7 %reshape.15 = f32[16,4,32,256]{3,2,1,0:T(8,128)S(1)} reshape(f32[16,4,8192]{2,1,0:T(4,128)} %all_to_all.9) | data formatting | bytes 4194304 | tf_op jit(solution)/shard_map/reshape | solution.py:279
  164.0 1.5 copy.7
  165.5 3.0 %copy.6 = f32[256,4,512]{2,1,0:T(4,128)} copy(f32[256,4,512]{0,2,1:T(8,128)} %bitcast.5) | data formatting | bytes 4194304

commit v5 on v4

--- a/solution.py
+++ b/solution.py
@@ -249,20 +249,24 @@
     bh = b.astype(jnp.bfloat16)
     bl = (b - bh.astype(f32)).astype(jnp.bfloat16)
     xh = xh_ref[...]
-    o_ref[...] = (jnp.dot(bh, xh, preferred_element_type=f32) + jnp.dot(bh, xl_ref[...], preferred_element_type=f32)
-                  + jnp.dot(bl, xh, preferred_element_type=f32))
-
-
-def project(basis_t, x_hi, x_lo, tile=1024):
+    res = (jnp.dot(bh, xh, preferred_element_type=f32) + jnp.dot(bh, xl_ref[...], preferred_element_type=f32)
+           + jnp.dot(bl, xh, preferred_element_type=f32))
+    width = o_ref.shape[2]
+    for jj in range(o_ref.shape[1]):
+        o_ref[:, jj, :] = res[:, jj * width:(jj + 1) * width]
+
+
+def project(basis_t, x_hi, x_lo, cols, depth, tile=2048):
     rank, rows = basis_t.shape
     width = x_hi.shape[1]
+    per = tile // depth
     return pl.pallas_call(
         _project_kernel,
-        out_shape=jax.ShapeDtypeStruct((rank, width), jnp.float32),
+        out_shape=jax.ShapeDtypeStruct((rank, cols, depth), jnp.float32),
         grid=(width // tile,),
         in_specs=[pl.BlockSpec((rank, rows), lambda g: (0, 0)),
                   pl.BlockSpec((rows, tile), lambda g: (0, g)), pl.BlockSpec((rows, tile), lambda g: (0, g))],
-        out_specs=pl.BlockSpec((rank, tile), lambda g: (0, g)),
+        out_specs=pl.BlockSpec((rank, per, depth), lambda g: (0, g, 0)),
     )(basis_t, x_hi, x_lo)
 
 
@@ -274,9 +278,9 @@
     gram_part, slab_hi, slab_lo = local_gram(tensor_slab)
     gram_full = allreduce_all(gram_part)
     basis = subspace_iterate(gram_full, start_basis)
-    proj = project(basis.T, slab_hi, slab_lo)
-    proj = lax.all_to_all(proj, "wide", split_axis=0, concat_axis=0, tiled=True)
-    core_unfold = proj.reshape(wide, -1, cols, depth).transpose(3, 1, 0, 2).reshape(depth, -1, wide * cols)
+    proj = project(basis.T, slab_hi, slab_lo, cols, depth)
+    proj = lax.all_to_all(proj, "wide", split_axis=0, concat_axis=1, tiled=True)
+    core_unfold = jnp.transpose(proj, (2, 0, 1))
     return (basis, core_unfold)
 
 

time: 169 us -> 160 us (0.947)
  local copies, waits for them, and re-layouts: 9.08 us -> 2.1 us
  Pallas kernels: 125 us -> 123 us
    reshape x2 -> x0, local copies, waits for them, and re-layouts: 4.18 us -> none  [shards(): proj.reshape(wide, -1, cols, depth).transpose(3, 1, 0, 2)]
    all_to_all x1, local copies, waits for them, and re-layouts: 1.86 us -> 0.14 us  [shards(): proj = lax.all_to_all(proj, 'wide', split_axis=0, concat_axis=1, tiled=True)]
where the time goes in v5:
time: 160 us
  Pallas kernels  123 us (77%)
  blocking collectives  33.9 us (21%)
  local copies, waits for them, and re-layouts  2.1 us (1%)
    pallas_call x1, Pallas kernels, subspace_iterate(): pl.pallas_call(_subspace_kernel, out_shape=jax.ShapeDtypeStruct(start_bas...  54.8 us
    pallas_call x1, Pallas kernels, allreduce_all(): pl.pallas_call(_allreduce_kernel, out_shape=jax.ShapeDtypeStruct((rows, c...  41.7 us
    all_to_all x1, blocking collectives, shards(): proj = lax.all_to_all(proj, 'wide', split_axis=0, concat_axis=1, tiled=True)  33.9 us
    pallas_call x1, Pallas kernels, local_gram(): pl.pallas_call(_gram_kernel, out_shape=(jax.ShapeDtypeStruct((rows, rows)...  17.5 us
    pallas_call x1, Pallas kernels, project(): pl.pallas_call(_project_kernel, out_shape=jax.ShapeDtypeStruct((rank, col...  9.55 us

profile of v5, /device:TPU:0, one launch (start us, length us, event | category | flops | bytes accessed | tf_op | source)
XLA Modules:
  0.0 160.1 jit_solution(2887931162653190654)
XLA Ops:
  0.6 17.5 %shard_map.41 = (f32[512,512]{1,0:T(8,128)}, bf16[512,8192]{1,0:T(8,128)(2,1)}, bf16[512,8192]{1,0:T(8,128)(2,1)}) custom-call(f32[512,32,256]{2,1,0:T(8,128)} %s_hbm.1), custom_call_target="tpu_custom_call" | custom-call | tf_op jit(solution)/shard_map/pallas_call | solution.py:229
  18.1 41.7 %shard_map.42.g_ref = f32[512,512]{1,0:T(8,128)} custom-call(f32[512,512]{1,0:T(8,128)} %get-tuple-element.5.x_ref), custom_call_target="tpu_custom_call" | custom-call | tf_op jit(solution)/shard_map/pallas_call | solution.py:112
  59.8 54.8 %shard_map.43.b_ref = f32[64,512]{1,0:T(8,128)} custom-call(f32[512,512]{1,0:T(8,128)} %shard_map.42.g_ref, f32[64,512]{1,0:T(8,128)} %bitcast.11), custom_call_target="tpu_custom_call" | custom-call | tf_op jit(solution)/shard_map/pallas_call | solution.py:170
  114.6 9.5 %shard_map.44 = f32[64,32,256]{2,1,0:T(8,128)} custom-call(f32[64,512]{1,0:T(8,128)} %shard_map.43.b_ref, bf16[512,8192]{1,0:T(8,128)(2,1)} %get-tuple-element.6.xh_ref, bf16[512,8192]{1,0:T(8,128)(2,1)} %get-tuple-element.7.xl_ref), custom_call_target="tpu_custom_call" | custom-call | tf_op jit(solution)/shard_map/pallas_call | solution.py:263
  124.1 33.9 %all_to_all.18 = f32[64,32,256]{2,1,0:T(8,128)S(1)} all-to-all(f32[64,32,256]{2,1,0:T(8,128)} %shard_map.44), channel_id=1, replica_groups=mesh['wide'=16,'narrow'=8] {'wide'}, dimensions={0} | all-to-all | bytes 4194304 | tf_op jit(solution)/shard_map/all_to_all | solution.py:282
  158.0 0.1 copy.5
  158.2 2.0 %copy.6 = f32[256,4,512]{2,1,0:T(4,128)} copy(f32[256,4,512]{0,2,1:T(8,128)S(1)} %bitcast.9) | data formatting | bytes 4194304

commit v6 on v5

--- a/solution.py
+++ b/solution.py
@@ -222,7 +222,7 @@
             cp.wait()
 
 
-def local_gram(slab, depth=8, slots=8):
+def local_gram(slab, depth=8, slots=16):
     rows, cols, width = slab.shape
     groups = cols // depth
     flat = jax.ShapeDtypeStruct((rows, cols * width), jnp.bfloat16)

time: 160 us -> 158 us (0.988)
    pallas_call x1, Pallas kernels: 17.5 us -> 15.6 us  [local_gram(): pl.pallas_call(_gram_kernel, out_shape=(jax.ShapeDtypeStruct((rows, rows)...]
where the time goes in v6:
time: 158 us
  Pallas kernels  122 us (77%)
  blocking collectives  33.9 us (21%)
  local copies, waits for them, and re-layouts  2.1 us (1%)
    pallas_call x1, Pallas kernels, subspace_iterate(): pl.pallas_call(_subspace_kernel, out_shape=jax.ShapeDtypeStruct(start_bas...  54.8 us
    pallas_call x1, Pallas kernels, allreduce_all(): pl.pallas_call(_allreduce_kernel, out_shape=jax.ShapeDtypeStruct((rows, c...  41.7 us
    all_to_all x1, blocking collectives, shards(): proj = lax.all_to_all(proj, 'wide', split_axis=0, concat_axis=1, tiled=True)  33.9 us
    pallas_call x1, Pallas kernels, local_gram(): pl.pallas_call(_gram_kernel, out_shape=(jax.ShapeDtypeStruct((rows, rows)...  15.6 us
    pallas_call x1, Pallas kernels, project(): pl.pallas_call(_project_kernel, out_shape=jax.ShapeDtypeStruct((rank, col...  9.55 us

profile of v6, /device:TPU:0, one launch (start us, length us, event | category | flops | bytes accessed | tf_op | source)
XLA Modules:
  0.0 158.2 jit_solution(17320253884785947213)
XLA Ops:
  0.6 15.6 %shard_map.41 = (f32[512,512]{1,0:T(8,128)}, bf16[512,8192]{1,0:T(8,128)(2,1)}, bf16[512,8192]{1,0:T(8,128)(2,1)}) custom-call(f32[512,32,256]{2,1,0:T(8,128)} %s_hbm.1), custom_call_target="tpu_custom_call" | custom-call | tf_op jit(solution)/shard_map/pallas_call | solution.py:229
  16.2 41.7 %shard_map.42.g_ref = f32[512,512]{1,0:T(8,128)} custom-call(f32[512,512]{1,0:T(8,128)} %get-tuple-element.5.x_ref), custom_call_target="tpu_custom_call" | custom-call | tf_op jit(solution)/shard_map/pallas_call | solution.py:112
  57.9 54.8 %shard_map.43.b_ref = f32[64,512]{1,0:T(8,128)} custom-call(f32[512,512]{1,0:T(8,128)} %shard_map.42.g_ref, f32[64,512]{1,0:T(8,128)} %bitcast.11), custom_call_target="tpu_custom_call" | custom-call | tf_op jit(solution)/shard_map/pallas_call | solution.py:170
  112.7 9.5 %shard_map.44 = f32[64,32,256]{2,1,0:T(8,128)} custom-call(f32[64,512]{1,0:T(8,128)} %shard_map.43.b_ref, bf16[512,8192]{1,0:T(8,128)(2,1)} %get-tuple-element.6.xh_ref, bf16[512,8192]{1,0:T(8,128)(2,1)} %get-tuple-element.7.xl_ref), custom_call_target="tpu_custom_call" | custom-call | tf_op jit(solution)/shard_map/pallas_call | solution.py:263
  122.2 33.9 %all_to_all.18 = f32[64,32,256]{2,1,0:T(8,128)S(1)} all-to-all(f32[64,32,256]{2,1,0:T(8,128)} %shard_map.44), channel_id=1, replica_groups=mesh['wide'=16,'narrow'=8] {'wide'}, dimensions={0} | all-to-all | bytes 4194304 | tf_op jit(solution)/shard_map/all_to_all | solution.py:282
  156.1 0.1 copy.5
  156.2 2.0 %copy.6 = f32[256,4,512]{2,1,0:T(4,128)} copy(f32[256,4,512]{0,2,1:T(8,128)S(1)} %bitcast.9) | data formatting | bytes 4194304

commit v7 on v6

--- a/solution.py
+++ b/solution.py
@@ -144,16 +144,20 @@
     def cholesky_inverse(m):
         e = eye
         z = zero
-        for j in range(rank):
-            row_m = m[j:j + 1, :]
-            col_m = m[:, j:j + 1]
-            s = lax.rsqrt(m[j:j + 1, j:j + 1])
-            c = jnp.where(col_idx >= j, col_m * s, 0.0)
-            r = jnp.where(row_idx >= j, row_m * s, 0.0)
-            m = m - c * r
-            zr = e[j:j + 1, :] * s
-            e = e - c * zr
-            z = jnp.where(rows == j, zr, z)
+        for j in range(0, rank, 2):
+            k = j + 1
+            s0 = lax.rsqrt(m[j:j + 1, j:j + 1])
+            t = m[j:j + 1, k:k + 1] * s0
+            c0 = jnp.where(col_idx >= j, m[:, j:j + 1] * s0, 0.0)
+            r0 = jnp.where(row_idx >= j, m[j:j + 1, :] * s0, 0.0)
+            s1 = lax.rsqrt(m[k:k + 1, k:k + 1] - t * t)
+            c1 = jnp.where(col_idx >= k, (m[:, k:k + 1] - c0 * t) * s1, 0.0)
+            r1 = jnp.where(row_idx >= k, (m[k:k + 1, :] - t * r0) * s1, 0.0)
+            m = m - c0 * r0 - c1 * r1
+            zj = e[j:j + 1, :] * s0
+            zk = (e[k:k + 1, :] - t * zj) * s1
+            e = e - c0 * zj - c1 * zk
+            z = jnp.where(rows == j, zj, jnp.where(rows == k, zk, z))
         return z
 
     def sweep(_, basis_t):

time: 158 us -> 188 us (1.19)
  Pallas kernels: 122 us -> 151 us
    pallas_call x1, Pallas kernels: 54.8 us -> 84.3 us  [subspace_iterate(): pl.pallas_call(_subspace_kernel, out_shape=jax.ShapeDtypeStruct(start_bas...]
where the time goes in v7:
time: 188 us
  Pallas kernels  151 us (80%)
  blocking collectives  33.9 us (18%)
  local copies, waits for them, and re-layouts  2.1 us (1%)
    pallas_call x1, Pallas kernels, subspace_iterate(): pl.pallas_call(_subspace_kernel, out_shape=jax.ShapeDtypeStruct(start_bas...  84.3 us
    pallas_call x1, Pallas kernels, allreduce_all(): pl.pallas_call(_allreduce_kernel, out_shape=jax.ShapeDtypeStruct((rows, c...  41.7 us
    all_to_all x1, blocking collectives, shards(): proj = lax.all_to_all(proj, 'wide', split_axis=0, concat_axis=1, tiled=True)  33.9 us
    pallas_call x1, Pallas kernels, local_gram(): pl.pallas_call(_gram_kernel, out_shape=(jax.ShapeDtypeStruct((rows, rows)...  15.6 us
    pallas_call x1, Pallas kernels, project(): pl.pallas_call(_project_kernel, out_shape=jax.ShapeDtypeStruct((rank, col...  9.55 us

profile of v7, /device:TPU:0, one launch (start us, length us, event | category | flops | bytes accessed | tf_op | source)
XLA Modules:
  0.0 187.7 jit_solution(222233450184174977)
XLA Ops:
  0.6 15.6 %shard_map.41 = (f32[512,512]{1,0:T(8,128)}, bf16[512,8192]{1,0:T(8,128)(2,1)}, bf16[512,8192]{1,0:T(8,128)(2,1)}) custom-call(f32[512,32,256]{2,1,0:T(8,128)} %s_hbm.1), custom_call_target="tpu_custom_call" | custom-call | tf_op jit(solution)/shard_map/pallas_call | solution.py:233
  16.2 41.7 %shard_map.42.g_ref = f32[512,512]{1,0:T(8,128)} custom-call(f32[512,512]{1,0:T(8,128)} %get-tuple-element.5.x_ref), custom_call_target="tpu_custom_call" | custom-call | tf_op jit(solution)/shard_map/pallas_call | solution.py:112
  57.9 84.3 %shard_map.43.b_ref = f32[64,512]{1,0:T(8,128)} custom-call(f32[512,512]{1,0:T(8,128)} %shard_map.42.g_ref, f32[64,512]{1,0:T(8,128)} %bitcast.11), custom_call_target="tpu_custom_call" | custom-call | tf_op jit(solution)/shard_map/pallas_call | solution.py:174
  142.2 9.5 %shard_map.44 = f32[64,32,256]{2,1,0:T(8,128)} custom-call(f32[64,512]{1,0:T(8,128)} %shard_map.43.b_ref, bf16[512,8192]{1,0:T(8,128)(2,1)} %get-tuple-element.6.xh_ref, bf16[512,8192]{1,0:T(8,128)(2,1)} %get-tuple-element.7.xl_ref), custom_call_target="tpu_custom_call" | custom-call | tf_op jit(solution)/shard_map/pallas_call | solution.py:267
  151.7 33.9 %all_to_all.18 = f32[64,32,256]{2,1,0:T(8,128)S(1)} all-to-all(f32[64,32,256]{2,1,0:T(8,128)} %shard_map.44), channel_id=1, replica_groups=mesh['wide'=16,'narrow'=8] {'wide'}, dimensions={0} | all-to-all | bytes 4194304 | tf_op jit(solution)/shard_map/all_to_all | solution.py:286
  185.6 0.1 copy.5
  185.7 2.0 %copy.6 = f32[256,4,512]{2,1,0:T(4,128)} copy(f32[256,4,512]{0,2,1:T(8,128)S(1)} %bitcast.9) | data formatting | bytes 4194304

commit v8 on v6

--- a/solution.py
+++ b/solution.py
@@ -132,7 +132,7 @@
 
 
 def _subspace_kernel(g_ref, b0_ref, o_ref):
-    highest = lax.Precision.HIGHEST
+    highest = lax.Precision.HIGH
     rank = b0_ref.shape[0]
     rows = lax.broadcasted_iota(jnp.int32, (rank, rank), 0)
     cols = lax.broadcasted_iota(jnp.int32, (rank, rank), 1)

time: 158 us -> 154 us (0.975)
  Pallas kernels: 122 us -> 118 us
    pallas_call x1, Pallas kernels: 54.8 us -> 50.8 us  [subspace_iterate(): pl.pallas_call(_subspace_kernel, out_shape=jax.ShapeDtypeStruct(start_bas...]
where the time goes in v8:
time: 154 us
  Pallas kernels  118 us (77%)
  blocking collectives  33.9 us (22%)
  local copies, waits for them, and re-layouts  2.1 us (1%)
    pallas_call x1, Pallas kernels, subspace_iterate(): pl.pallas_call(_subspace_kernel, out_shape=jax.ShapeDtypeStruct(start_bas...  50.8 us
    pallas_call x1, Pallas kernels, allreduce_all(): pl.pallas_call(_allreduce_kernel, out_shape=jax.ShapeDtypeStruct((rows, c...  41.7 us
    all_to_all x1, blocking collectives, shards(): proj = lax.all_to_all(proj, 'wide', split_axis=0, concat_axis=1, tiled=True)  33.9 us
    pallas_call x1, Pallas kernels, local_gram(): pl.pallas_call(_gram_kernel, out_shape=(jax.ShapeDtypeStruct((rows, rows)...  15.6 us
    pallas_call x1, Pallas kernels, project(): pl.pallas_call(_project_kernel, out_shape=jax.ShapeDtypeStruct((rank, col...  9.55 us

profile of v8, /device:TPU:0, one launch (start us, length us, event | category | flops | bytes accessed | tf_op | source)
XLA Modules:
  0.0 154.2 jit_solution(15468410349732448315)
XLA Ops:
  0.6 15.6 %shard_map.41 = (f32[512,512]{1,0:T(8,128)}, bf16[512,8192]{1,0:T(8,128)(2,1)}, bf16[512,8192]{1,0:T(8,128)(2,1)}) custom-call(f32[512,32,256]{2,1,0:T(8,128)} %s_hbm.1), custom_call_target="tpu_custom_call" | custom-call | tf_op jit(solution)/shard_map/pallas_call | solution.py:229
  16.2 41.7 %shard_map.42.g_ref = f32[512,512]{1,0:T(8,128)} custom-call(f32[512,512]{1,0:T(8,128)} %get-tuple-element.5.x_ref), custom_call_target="tpu_custom_call" | custom-call | tf_op jit(solution)/shard_map/pallas_call | solution.py:112
  57.9 50.8 %shard_map.43.b_ref = f32[64,512]{1,0:T(8,128)} custom-call(f32[512,512]{1,0:T(8,128)} %shard_map.42.g_ref, f32[64,512]{1,0:T(8,128)} %bitcast.11), custom_call_target="tpu_custom_call" | custom-call | tf_op jit(solution)/shard_map/pallas_call | solution.py:170
  108.6 9.5 %shard_map.44 = f32[64,32,256]{2,1,0:T(8,128)} custom-call(f32[64,512]{1,0:T(8,128)} %shard_map.43.b_ref, bf16[512,8192]{1,0:T(8,128)(2,1)} %get-tuple-element.6.xh_ref, bf16[512,8192]{1,0:T(8,128)(2,1)} %get-tuple-element.7.xl_ref), custom_call_target="tpu_custom_call" | custom-call | tf_op jit(solution)/shard_map/pallas_call | solution.py:263
  118.2 33.9 %all_to_all.18 = f32[64,32,256]{2,1,0:T(8,128)S(1)} all-to-all(f32[64,32,256]{2,1,0:T(8,128)} %shard_map.44), channel_id=1, replica_groups=mesh['wide'=16,'narrow'=8] {'wide'}, dimensions={0} | all-to-all | bytes 4194304 | tf_op jit(solution)/shard_map/all_to_all | solution.py:282
  152.1 0.1 copy.5
  152.2 2.0 %copy.6 = f32[256,4,512]{2,1,0:T(4,128)} copy(f32[256,4,512]{0,2,1:T(8,128)S(1)} %bitcast.9) | data formatting | bytes 4194304

commit v9 on v6

--- a/solution.py
+++ b/solution.py
@@ -222,7 +222,7 @@
             cp.wait()
 
 
-def local_gram(slab, depth=8, slots=16):
+def local_gram(slab, depth=16, slots=16):
     rows, cols, width = slab.shape
     groups = cols // depth
     flat = jax.ShapeDtypeStruct((rows, cols * width), jnp.bfloat16)

time: 158 us -> 160 us (1.013)
  no operation moved by 1% of the time
where the time goes in v9:
time: 160 us; the launch traced here: 159 us
  Pallas kernels  123 us (77%)
  blocking collectives  33.9 us (21%)
  local copies, waits for them, and re-layouts  2.1 us (1%)
    pallas_call x1, Pallas kernels, subspace_iterate(): pl.pallas_call(_subspace_kernel, out_shape=jax.ShapeDtypeStruct(start_bas...  54.8 us
    pallas_call x1, Pallas kernels, allreduce_all(): pl.pallas_call(_allreduce_kernel, out_shape=jax.ShapeDtypeStruct((rows, c...  41.7 us
    all_to_all x1, blocking collectives, shards(): proj = lax.all_to_all(proj, 'wide', split_axis=0, concat_axis=1, tiled=True)  33.9 us
    pallas_call x1, Pallas kernels, local_gram(): pl.pallas_call(_gram_kernel, out_shape=(jax.ShapeDtypeStruct((rows, rows)...  16.7 us
    pallas_call x1, Pallas kernels, project(): pl.pallas_call(_project_kernel, out_shape=jax.ShapeDtypeStruct((rank, col...  9.55 us

profile of v9, /device:TPU:0, one launch (start us, length us, event | category | flops | bytes accessed | tf_op | source)
XLA Modules:
  0.0 159.4 jit_solution(13746321619042885840)
XLA Ops:
  0.6 16.7 %shard_map.41 = (f32[512,512]{1,0:T(8,128)}, bf16[512,8192]{1,0:T(8,128)(2,1)}, bf16[512,8192]{1,0:T(8,128)(2,1)}) custom-call(f32[512,32,256]{2,1,0:T(8,128)} %s_hbm.1), custom_call_target="tpu_custom_call" | custom-call | tf_op jit(solution)/shard_map/pallas_call | solution.py:229
  17.4 41.7 %shard_map.42.g_ref = f32[512,512]{1,0:T(8,128)} custom-call(f32[512,512]{1,0:T(8,128)} %get-tuple-element.5.x_ref), custom_call_target="tpu_custom_call" | custom-call | tf_op jit(solution)/shard_map/pallas_call | solution.py:112
  59.0 54.8 %shard_map.43.b_ref = f32[64,512]{1,0:T(8,128)} custom-call(f32[512,512]{1,0:T(8,128)} %shard_map.42.g_ref, f32[64,512]{1,0:T(8,128)} %bitcast.11), custom_call_target="tpu_custom_call" | custom-call | tf_op jit(solution)/shard_map/pallas_call | solution.py:170
  113.8 9.5 %shard_map.44 = f32[64,32,256]{2,1,0:T(8,128)} custom-call(f32[64,512]{1,0:T(8,128)} %shard_map.43.b_ref, bf16[512,8192]{1,0:T(8,128)(2,1)} %get-tuple-element.6.xh_ref, bf16[512,8192]{1,0:T(8,128)(2,1)} %get-tuple-element.7.xl_ref), custom_call_target="tpu_custom_call" | custom-call | tf_op jit(solution)/shard_map/pallas_call | solution.py:263
  123.4 33.9 %all_to_all.18 = f32[64,32,256]{2,1,0:T(8,128)S(1)} all-to-all(f32[64,32,256]{2,1,0:T(8,128)} %shard_map.44), channel_id=1, replica_groups=mesh['wide'=16,'narrow'=8] {'wide'}, dimensions={0} | all-to-all | bytes 4194304 | tf_op jit(solution)/shard_map/all_to_all | solution.py:282
  157.3 0.1 copy.5
  157.4 2.0 %copy.6 = f32[256,4,512]{2,1,0:T(4,128)} copy(f32[256,4,512]{0,2,1:T(8,128)S(1)} %bitcast.9) | data formatting | bytes 4194304

commit v10 on v9

--- a/solution.py
+++ b/solution.py
@@ -222,7 +222,7 @@
             cp.wait()
 
 
-def local_gram(slab, depth=16, slots=16):
+def local_gram(slab, depth=8, slots=32):
     rows, cols, width = slab.shape
     groups = cols // depth
     flat = jax.ShapeDtypeStruct((rows, cols * width), jnp.bfloat16)

time: 160 us -> 158 us (0.988)
  no operation moved by 1% of the time
where the time goes in v10:
time: 158 us
  Pallas kernels  122 us (77%)
  blocking collectives  33.9 us (21%)
  local copies, waits for them, and re-layouts  2.1 us (1%)
    pallas_call x1, Pallas kernels, subspace_iterate(): pl.pallas_call(_subspace_kernel, out_shape=jax.ShapeDtypeStruct(start_bas...  54.8 us
    pallas_call x1, Pallas kernels, allreduce_all(): pl.pallas_call(_allreduce_kernel, out_shape=jax.ShapeDtypeStruct((rows, c...  41.7 us
    all_to_all x1, blocking collectives, shards(): proj = lax.all_to_all(proj, 'wide', split_axis=0, concat_axis=1, tiled=True)  33.9 us
    pallas_call x1, Pallas kernels, local_gram(): pl.pallas_call(_gram_kernel, out_shape=(jax.ShapeDtypeStruct((rows, rows)...  15.6 us
    pallas_call x1, Pallas kernels, project(): pl.pallas_call(_project_kernel, out_shape=jax.ShapeDtypeStruct((rank, col...  9.55 us

profile of v10, /device:TPU:0, one launch (start us, length us, event | category | flops | bytes accessed | tf_op | source)
XLA Modules:
  0.0 158.3 jit_solution(7993361804406528235)
XLA Ops:
  0.6 15.6 %shard_map.41 = (f32[512,512]{1,0:T(8,128)}, bf16[512,8192]{1,0:T(8,128)(2,1)}, bf16[512,8192]{1,0:T(8,128)(2,1)}) custom-call(f32[512,32,256]{2,1,0:T(8,128)} %s_hbm.1), custom_call_target="tpu_custom_call" | custom-call | tf_op jit(solution)/shard_map/pallas_call | solution.py:229
  16.3 41.7 %shard_map.42.g_ref = f32[512,512]{1,0:T(8,128)} custom-call(f32[512,512]{1,0:T(8,128)} %get-tuple-element.5.x_ref), custom_call_target="tpu_custom_call" | custom-call | tf_op jit(solution)/shard_map/pallas_call | solution.py:112
  57.9 54.8 %shard_map.43.b_ref = f32[64,512]{1,0:T(8,128)} custom-call(f32[512,512]{1,0:T(8,128)} %shard_map.42.g_ref, f32[64,512]{1,0:T(8,128)} %bitcast.11), custom_call_target="tpu_custom_call" | custom-call | tf_op jit(solution)/shard_map/pallas_call | solution.py:170
  112.7 9.5 %shard_map.44 = f32[64,32,256]{2,1,0:T(8,128)} custom-call(f32[64,512]{1,0:T(8,128)} %shard_map.43.b_ref, bf16[512,8192]{1,0:T(8,128)(2,1)} %get-tuple-element.6.xh_ref, bf16[512,8192]{1,0:T(8,128)(2,1)} %get-tuple-element.7.xl_ref), custom_call_target="tpu_custom_call" | custom-call | tf_op jit(solution)/shard_map/pallas_call | solution.py:263
  122.3 33.9 %all_to_all.18 = f32[64,32,256]{2,1,0:T(8,128)S(1)} all-to-all(f32[64,32,256]{2,1,0:T(8,128)} %shard_map.44), channel_id=1, replica_groups=mesh['wide'=16,'narrow'=8] {'wide'}, dimensions={0} | all-to-all | bytes 4194304 | tf_op jit(solution)/shard_map/all_to_all | solution.py:282
  156.2 0.1 copy.5
  156.3 2.0 %copy.6 = f32[256,4,512]{2,1,0:T(4,128)} copy(f32[256,4,512]{0,2,1:T(8,128)S(1)} %bitcast.9) | data formatting | bytes 4194304
